TPU v7x, 32 devices: a whole 2x2x4 slice. The times are simulated.
32 devices in a mesh: seq: 4 (over y, x), ctx: 4 (over z), fsdp: 2 (over core).
Axes of the slice: x: 2, y: 2, z: 4, core: 2. Of those that a mesh axis runs over, the one named last changes fastest.
Arguments:
- inputs: bfloat16 [8, 512, 2048], P(('seq', 'fsdp'), 'ctx'), may hold values from -6 to 6
- block_index: int32 [8, 4, 2], P(('seq', 'fsdp'), 'ctx'), may hold values from 0 to 7, as said below
- attention_gain: float32 [2048], replicated, may hold values from 0.1 to 1.9
- query_norm_gain: float32 [128], replicated, may hold values from 0.1 to 1.9
- key_gain: float32 [128], replicated, may hold values from 0.1 to 1.9
- feedforward_gain: float32 [2048], replicated, may hold values from 0.1 to 1.9
- attention_in: bfloat16 [2048, 4096], P(('seq', 'fsdp')), may hold values from -0.125 to 0.125
- attention_out: bfloat16 [2048, 2048], P(('seq', 'fsdp')), may hold values from -0.75 to 0.75
- gate_up: bfloat16 [2048, 12288], P(('seq', 'fsdp')), may hold values from -0.125 to 0.125
- down_weight: bfloat16 [2048, 6144], P(('seq', 'fsdp')), may hold values from -0.078125 to 0.078125
- grad_output: bfloat16 [8, 512, 2048], P(('seq', 'fsdp'), 'ctx'), may hold values from -6 to 6
Outputs:
- output: bfloat16 [8, 512, 2048], P(('seq', 'fsdp'), 'ctx')
- input_grad: bfloat16 [8, 512, 2048], P(('seq', 'fsdp'), 'ctx')
- attention_gain_grad: float32 [2048], replicated
- query_gain_grad: float32 [128], replicated
- key_gain_grad: float32 [128], replicated
- feedforward_gain_grad: float32 [2048], replicated
- attention_in_grad: float32 [2048, 4096], P(('seq', 'ctx', 'fsdp'))
- attention_out_grad: float32 [2048, 2048], P(('seq', 'ctx', 'fsdp'))
- gate_up_grad: float32 [2048, 12288], P(('seq', 'ctx', 'fsdp'))
- down_grad: float32 [2048, 6144], P(('seq', 'ctx', 'fsdp'))
Inputs may be any that keep to these rules, and one draw needn't show every extreme that they name: For each sequence s, block_index[s, c, 0] over c takes each of 0 to 3 once, and block_index[s, c, 1] = 7 - block_index[s, c, 0].
All inputs are finite; a program needn't handle non-finite values.
Results may differ from a plain program's by a relative error of at most 0.018.
Values may be sent and summed in bfloat16 or wider, within the bound.
No kernel may reach another device: no remote copies, remote signals or barrier semaphores. Data moves between devices by JAX's collectives and lax.ppermute only.
A program may use at most 832 MiB of HBM per device.

v0:
```python
import jax
import jax.numpy as jnp
from jax import lax
from jax.sharding import PartitionSpec as P

D = 2048
QUERY_HEADS = 16
KEY_VALUE_HEADS = 8
HEAD_SIZE = 128
FF = 6144
EPS = 1e-06
ROPE_BASE = 1000000.0
MASK_FLOOR = -1e30
PLANE = ("seq", "fsdp")
F32 = jnp.float32
BF16 = jnp.bfloat16


def rms_scale(values):
    return lax.rsqrt(jnp.mean(values * values, axis=-1, keepdims=True) + EPS)


def rms_back(grad_normed, normed_hat, scale, gain):
    grad_hat = grad_normed * gain
    inner = jnp.mean(grad_hat * normed_hat, axis=-1, keepdims=True)
    return scale * (grad_hat - normed_hat * inner)


def rope_tables(token_positions):
    half = HEAD_SIZE // 2
    rates = jnp.power(F32(ROPE_BASE), jnp.arange(half, dtype=F32) * (-2.0 / HEAD_SIZE))
    angles = token_positions.astype(F32)[:, None] * rates[None, :]
    angles = jnp.concatenate([angles, angles], axis=1)
    return (jnp.cos(angles), jnp.sin(angles))


def apply_rotation(values, cosine_table, sine_table):
    half = values.shape[-1] // 2
    turned = jnp.concatenate([-values[..., half:], values[..., :half]], axis=-1)
    return values * cosine_table[:, None, :] + turned * sine_table[:, None, :]


def rotate_back(grads, cosine_table, sine_table):
    half = grads.shape[-1] // 2
    scaled = grads * sine_table[:, None, :]
    turned = jnp.concatenate([scaled[..., half:], -scaled[..., :half]], axis=-1)
    return grads * cosine_table[:, None, :] + turned


def rows_by(left, right):
    return jnp.dot(left, right, preferred_element_type=F32)


def rows_by_t(left, right):
    return lax.dot_general(left, right, (((1,), (1,)), ((), ())), preferred_element_type=F32)


def t_by_rows(left, right):
    return lax.dot_general(left, right, (((0,), (0,)), ((), ())), preferred_element_type=F32)


def gather_ctx(rows):
    return lax.all_gather(rows, "ctx", axis=0, tiled=True)


def gather_plane(rows):
    return lax.all_gather(rows, PLANE, axis=0, tiled=True)


def scatter_ctx(partials):
    parts = lax.axis_size("ctx")
    pieces = lax.all_to_all(partials.astype(BF16), "ctx", 0, 0, tiled=True)
    pieces = pieces.reshape(parts, partials.shape[0] // parts, partials.shape[1])
    return jnp.sum(pieces.astype(F32), axis=0)


def scatter_weight(grad):
    seqs, ctxs, cores = (lax.axis_size("seq"), lax.axis_size("ctx"), lax.axis_size("fsdp"))
    rows = grad.shape[0] // (seqs * ctxs * cores)
    grad = grad.astype(BF16).reshape(seqs, ctxs, cores, rows, grad.shape[1])
    grad = jnp.transpose(grad, (0, 2, 1, 3, 4)).reshape(-1, grad.shape[-1])
    grad = lax.psum_scatter(grad, PLANE, scatter_dimension=0, tiled=True)
    grad = lax.all_to_all(grad, "ctx", 0, 0, tiled=True)
    return grad.reshape(ctxs, rows, grad.shape[-1])


def join_columns(pieces):
    parts, rows, width = pieces.shape
    return jnp.transpose(pieces, (1, 0, 2)).reshape(rows, parts * width).astype(F32)


def local(
    inputs,
    block_index,
    attention_gain,
    query_norm_gain,
    key_gain,
    feedforward_gain,
    attention_in,
    attention_out,
    gate_up,
    down_weight,
    grad_output,
):
    parts = lax.axis_size("ctx")
    me = lax.axis_index("ctx")
    tokens = inputs.shape[1]
    half_rows = tokens // 2
    length = tokens * parts
    query_heads = QUERY_HEADS // parts
    key_heads = max(1, KEY_VALUE_HEADS // parts)
    copies = key_heads * parts // KEY_VALUE_HEADS
    group = query_heads // key_heads
    query_width = query_heads * HEAD_SIZE
    key_width = key_heads * HEAD_SIZE
    all_query = QUERY_HEADS * HEAD_SIZE
    all_key = KEY_VALUE_HEADS * HEAD_SIZE
    hidden_width = FF // parts
    scale = HEAD_SIZE ** (-0.5)

    def columns(weight, start, width):
        return lax.dynamic_slice_in_dim(weight, start, width, axis=1)

    key_start = me // copies * key_width
    weight_in = gather_plane(
        jnp.concatenate(
            [
                columns(attention_in, me * query_width, query_width),
                columns(attention_in, all_query + key_start, key_width),
                columns(attention_in, all_query + all_key + key_start, key_width),
            ],
            axis=1,
        )
    )
    own_inputs = inputs[0]
    sequence_inputs = gather_ctx(own_inputs)
    blocks = lax.all_gather(block_index[0, 0], "ctx", axis=0, tiled=True)
    weight_out = gather_plane(attention_out)
    weight_gate_up = gather_plane(
        jnp.concatenate(
            [
                columns(gate_up, me * hidden_width, hidden_width),
                columns(gate_up, FF + me * hidden_width, hidden_width),
            ],
            axis=1,
        )
    )
    weight_down = gather_plane(columns(down_weight, me * hidden_width, hidden_width))
    own_grad = grad_output[0]
    sequence_grad = gather_ctx(own_grad)
    steps_along = jnp.arange(half_rows, dtype=jnp.int32)
    positions = (blocks[:, None] * half_rows + steps_along[None, :]).reshape(-1)
    cosine_table, sine_table = rope_tables(positions)
    rows = sequence_inputs.astype(F32)
    first_scale = rms_scale(rows)
    first_hat = rows * first_scale
    first_normed = (first_hat * attention_gain).astype(BF16)
    projected = rows_by(first_normed, weight_in)
    query = projected[:, :query_width].reshape(length, query_heads, HEAD_SIZE)
    key = projected[:, query_width : query_width + key_width].reshape(length, key_heads, HEAD_SIZE)
    value = projected[:, query_width + key_width :].astype(BF16)
    value = value.reshape(length, key_heads, HEAD_SIZE)
    query_scale = rms_scale(query)
    query_hat = query * query_scale
    key_scale = rms_scale(key)
    key_hat = key * key_scale
    rotary_query = (
        apply_rotation(query_hat * query_norm_gain, cosine_table, sine_table)
        .astype(BF16)
        .reshape(length, key_heads, group, HEAD_SIZE)
    )
    rotary_key = apply_rotation(key_hat * key_gain, cosine_table, sine_table).astype(BF16)
    scores = (
        jnp.einsum("qhgd,khd->hgqk", rotary_query, rotary_key, preferred_element_type=F32) * scale
    )
    allowed = positions[None, :] <= positions[:, None]
    scores = jnp.where(allowed, scores, MASK_FLOOR)
    peak = jnp.max(scores, axis=-1, keepdims=True)
    total = jnp.sum(jnp.where(allowed, jnp.exp(scores - peak), 0.0), axis=-1, keepdims=True)
    total_logarithm = peak + jnp.log(total)
    probs = jnp.where(allowed, jnp.exp(scores - total_logarithm), 0.0)
    weights = probs.astype(BF16)
    attended = jnp.einsum("hgqk,khd->qhgd", weights, value, preferred_element_type=F32)
    attended = attended.astype(BF16).reshape(length, query_width)
    own_attended = lax.all_to_all(attended, "ctx", 0, 1, tiled=True)
    own_rows = own_inputs.astype(F32)
    middle = own_rows + rows_by_t(own_attended, weight_out)
    second_scale = rms_scale(middle)
    second_hat = middle * second_scale
    second_normed = (second_hat * feedforward_gain).astype(BF16)
    sequence_second = gather_ctx(second_normed)
    grad_hidden = rows_by(sequence_grad, weight_down)
    gate_values = rows_by(sequence_second, weight_gate_up)
    gate = gate_values[:, :hidden_width]
    upward = gate_values[:, hidden_width:]
    sigmoid_gate = jax.nn.sigmoid(gate)
    silu_gate = gate * sigmoid_gate
    hidden = (silu_gate * upward).astype(BF16)
    grad_gate = grad_hidden * upward * sigmoid_gate * (1.0 + gate * (1.0 - sigmoid_gate))
    grad_upward = grad_hidden * silu_gate
    grad_gate_up = jnp.concatenate([grad_gate, grad_upward], axis=1).astype(BF16)
    grad_second = scatter_ctx(rows_by_t(grad_gate_up, weight_gate_up))
    down_pieces = scatter_weight(t_by_rows(sequence_grad, hidden))
    gate_up_pieces = scatter_weight(t_by_rows(sequence_second, grad_gate_up))
    output = middle + scatter_ctx(rows_by_t(hidden, weight_down))
    feedforward_part = jnp.sum(grad_second * second_hat, axis=0)
    grad_middle = own_grad.astype(F32) + rms_back(
        grad_second, second_hat, second_scale, feedforward_gain
    )
    grad_middle_short = grad_middle.astype(BF16)
    own_attended_grad = rows_by(grad_middle_short, weight_out).astype(BF16)
    attended_grad = lax.all_to_all(own_attended_grad, "ctx", 1, 0, tiled=True)
    sequence_middle_grad = gather_ctx(grad_middle_short)
    out_pieces = scatter_weight(t_by_rows(sequence_middle_grad, attended))
    delta = jnp.sum(
        (attended_grad.astype(F32) * attended.astype(F32)).reshape(
            length, key_heads, group, HEAD_SIZE
        ),
        axis=-1,
    )
    head_grads = attended_grad.reshape(length, key_heads, group, HEAD_SIZE)
    grad_probs = jnp.einsum("qhgd,khd->hgqk", head_grads, value, preferred_element_type=F32)
    grad_scores = (probs * (grad_probs - jnp.transpose(delta, (1, 2, 0))[..., None])).astype(BF16)
    grad_rotary_query = (
        jnp.einsum("hgqk,khd->qhgd", grad_scores, rotary_key, preferred_element_type=F32) * scale
    )
    grad_rotary_key = (
        jnp.einsum("hgqk,qhgd->khd", grad_scores, rotary_query, preferred_element_type=F32) * scale
    )
    value_grad = jnp.einsum("hgqk,qhgd->khd", weights, head_grads, preferred_element_type=F32)
    unrotated_query = rotate_back(
        grad_rotary_query.reshape(length, query_heads, HEAD_SIZE), cosine_table, sine_table
    )
    unrotated_key = rotate_back(grad_rotary_key, cosine_table, sine_table)
    query_part = jnp.sum(unrotated_query * query_hat, axis=(0, 1))
    key_part = jnp.sum(unrotated_key * key_hat, axis=(0, 1))
    grad_query = rms_back(unrotated_query, query_hat, query_scale, query_norm_gain)
    grad_key = rms_back(unrotated_key, key_hat, key_scale, key_gain)
    grad_projected = jnp.concatenate(
        [
            grad_query.reshape(length, query_width),
            grad_key.reshape(length, key_width),
            value_grad.reshape(length, key_width),
        ],
        axis=1,
    ).astype(BF16)
    partial_first = rows_by_t(grad_projected, weight_in)
    attention_part = jnp.sum(partial_first * first_hat, axis=0)
    grad_first = scatter_ctx(partial_first)
    in_pieces = scatter_weight(t_by_rows(first_normed, grad_projected))
    own_scale = rms_scale(own_rows)
    input_grad = grad_middle + rms_back(grad_first, own_rows * own_scale, own_scale, attention_gain)
    gain_sums = lax.psum(
        (attention_part, query_part, key_part, feedforward_part), ("seq", "ctx", "fsdp")
    )

    def merge_copies(pieces):
        shape = pieces.shape
        return jnp.sum(pieces.reshape(shape[0] // copies, copies, shape[1], shape[2]), axis=1)

    attention_in_grad = jnp.concatenate(
        [
            join_columns(in_pieces[:, :, :query_width]),
            join_columns(
                merge_copies(in_pieces[:, :, query_width : query_width + key_width].astype(F32))
            ),
            join_columns(merge_copies(in_pieces[:, :, query_width + key_width :].astype(F32))),
        ],
        axis=1,
    )
    gate_up_grad = jnp.concatenate(
        [
            join_columns(gate_up_pieces[:, :, :hidden_width]),
            join_columns(gate_up_pieces[:, :, hidden_width:]),
        ],
        axis=1,
    )
    return (
        output.astype(BF16)[None],
        input_grad.astype(BF16)[None],
        gain_sums[0],
        gain_sums[1],
        gain_sums[2],
        gain_sums[3],
        attention_in_grad,
        join_columns(out_pieces),
        gate_up_grad,
        join_columns(down_pieces),
    )


def solution(mesh):
    tokens = P(("seq", "fsdp"), "ctx", None)
    weight = P(("seq", "fsdp"), None)
    grad = P(("seq", "ctx", "fsdp"), None)
    in_specs = (tokens, tokens, P(), P(), P(), P(), weight, weight, weight, weight, tokens)
    out_specs = (tokens, tokens, P(), P(), P(), P(), grad, grad, grad, grad)
    return jax.shard_map(local, mesh=mesh, in_specs=in_specs, out_specs=out_specs, check_vma=False)
```

profile of v0, /device:TPU:0, one launch (start us, length us, event | category | flops | bytes accessed | tf_op | source)
XLA Modules:
  0.0 858.8 jit_solution(17743608366235928111)
XLA Ops:
  13.2 10.0 %all-reduce = s32[8]{0:T(128)S(1)} all-reduce(s32[8]{0:T(128)S(1)} %bitcast_dynamic-update-slice_fusion), channel_id=3, replica_groups=mesh['seq'=4,'ctx'=4,'fsdp'=2] {'ctx'}, use_global_device_ids=true, to_apply=%add | all-reduce | flops 8 | bytes 64
  25.5 32.6 %all-gather.24.cloned.1.call-done = bf16[1,512,2048]{2,1,0:T(8,128)(2,1)} async-done(((bf16[1,128,2048]{2,1,0:T(8,128)(2,1)}), bf16[1,512,2048]{2,1,0:T(8,128)(2,1)}) %all-gather.24.cloned.1.call-update) | async-done | bytes 2097168 | tf_op jit(solution)/shard_map/all_gather | solution.py:63
  60.1 35.7 %all-gather.12.cloned.1.call-done = bf16[2048,1024]{1,0:T(8,128)(2,1)} async-done(((bf16[256,1024]{1,0:T(8,128)(2,1)}), bf16[2048,1024]{1,0:T(8,128)(2,1)}) %all-gather.12.cloned.1.call-update) | async-done | bytes 4194320 | tf_op jit(solution)/shard_map/all_gather | solution.py:67
  128.9 19.6 %all_to_all.98 = bf16[4,128,512]{1,2,0:T(8,128)(2,1)} all-to-all(bf16[4,128,512]{1,2,0:T(8,128)(2,1)S(1)} %copy.204), channel_id=1, replica_groups=mesh['seq'=4,'ctx'=4,'fsdp'=2] {'ctx'}, dimensions={0} | all-to-all | bytes 1048576 | tf_op jit(solution)/shard_map/all_to_all | solution.py:185
  165.1 41.2 %all-gather.16.cloned.1.call-done = bf16[512,2048]{1,0:T(8,128)(2,1)} async-done(((bf16[128,2048]{1,0:T(8,128)(2,1)}), bf16[512,2048]{1,0:T(8,128)(2,1)}) %all-gather.16.cloned.1.call-update) | async-done | bytes 2097168 | tf_op jit(solution)/shard_map/all_gather | solution.py:63
  206.3 73.1 %all-gather.18.cloned.1.call-done = bf16[2048,3072]{1,0:T(8,128)(2,1)} async-done(((bf16[256,3072]{1,0:T(8,128)(2,1)}), bf16[2048,3072]{1,0:T(8,128)(2,1)}) %all-gather.18.cloned.1.call-update) | async-done | bytes 12582928 | tf_op jit(solution)/shard_map/all_gather | solution.py:67
  279.5 11.9 %fusion.50 = f32[512,3072]{1,0:T(8,128)} fusion(bf16[512,2048]{1,0:T(8,128)(2,1)} %all-gather.16.cloned.1.call-done, bf16[2048,3072]{1,0:T(8,128)(2,1)} %all-gather.18.cloned.1.call-done), kind=kOutput, calls=%fused_computation.145 | convolution fusion | flops 6442450944 | bytes 20971520 | tf_op jit(solution)/shard_map/dot_general | solution.py:51
  291.4 35.2 %all-gather.26.cloned.1.call-done = bf16[1,512,2048]{2,1,0:T(8,128)(2,1)} async-done(((bf16[1,128,2048]{2,1,0:T(8,128)(2,1)}), bf16[1,512,2048]{2,1,0:T(8,128)(2,1)}) %all-gather.26.cloned.1.call-update) | async-done | bytes 2097168 | tf_op jit(solution)/shard_map/all_gather | solution.py:63
  326.6 46.7 %all-gather.20.cloned.1.call-done = bf16[2048,1536]{1,0:T(8,128)(2,1)} async-done(((bf16[256,1536]{1,0:T(8,128)(2,1)}), bf16[2048,1536]{1,0:T(8,128)(2,1)}) %all-gather.20.cloned.1.call-update) | async-done | bytes 6291472 | tf_op jit(solution)/shard_map/all_gather | solution.py:67
  373.3 10.9 %multiply_convert_fusion.1 = (bf16[512,1536]{1,0:T(8,128)(2,1)S(1)}, bf16[512,1536]{1,0:T(8,128)(2,1)S(1)}, bf16[512,1536]{1,0:T(8,128)(2,1)}) fusion(f32[512,3072]{1,0:T(8,128)} %fusion.50, bf16[2048,1536]{1,0:T(8,128)(2,1)} %all-gather.20.cloned.1.call-done, bf16[1,512,2048]{2,1,0:T(8,128)(2,1)} %all-gather.26.cloned.1.call-done), kind=kOutput, calls=%fused_computation.24 | convolution fusion | flops 3233021952 | bytes 19398656 | tf_op jit(solution)/shard_map/dot_general | solution.py:51
  384.2 6.9 convolution_convert_fusion.3
  391.1 53.1 %all_to_all.99 = bf16[4,128,2048]{2,1,0:T(8,128)(2,1)S(1)} all-to-all(bf16[4,128,2048]{2,1,0:T(8,128)(2,1)S(1)} %bitcast.232), channel_id=1, replica_groups=mesh['seq'=4,'ctx'=4,'fsdp'=2] {'ctx'}, dimensions={0} | all-to-all | bytes 4194304 | tf_op jit(solution)/shard_map/all_to_all | solution.py:72
  446.7 43.7 %all-gather.22.cloned.1.call-done = bf16[512,2048]{1,0:T(8,128)(2,1)} async-done(((bf16[128,2048]{1,0:T(8,128)(2,1)}), bf16[512,2048]{1,0:T(8,128)(2,1)}) %all-gather.22.cloned.1.call-update) | async-done | bytes 2097168 | tf_op jit(solution)/shard_map/all_gather | solution.py:63
  494.9 8.2 fusion
  503.1 8.7 %copy.233 = bf16[2048,1536]{1,0:T(8,128)(2,1)} copy(bf16[2048,1536]{0,1:T(8,128)(2,1)} %fusion) | data formatting | bytes 12582912 | tf_op jit(solution)/shard_map/convert_element_type | solution.py:80
  534.3 11.1 %all-to-all-done.3 = bf16[128,4,512]{0,2,1:T(8,128)(2,1)} async-done(((bf16[128,4,512]{0,2,1:T(8,128)(2,1)}), bf16[128,4,512]{0,2,1:T(8,128)(2,1)}, u32[]{:S(2)}, u32[]{:S(2)}) %all-to-all-start.3) | async-done | bytes 524320 | tf_op jit(solution)/shard_map/all_to_all | solution.py:212
  592.2 9.2 %convolution_convert_fusion = bf16[2048,3072]{1,0:T(8,128)(2,1)S(1)} fusion(bf16[512,2048]{1,0:T(8,128)(2,1)} %all-gather.16.cloned.1.call-done, bf16[512,1536]{1,0:T(8,128)(2,1)} %copy-done.47, bf16[512,1536]{1,0:T(8,128)(2,1)} %copy-done.46), kind=kOutput, calls=%fused_computation | convolution fusion | flops 6455033856 | bytes 17825792 | tf_op jit(solution)/shard_map/dot_general | solution.py:59
  607.1 8.4 convolution_convert_fusion.5
  626.8 41.7 %all-to-all-done.1 = bf16[4,128,2048]{2,1,0:T(8,128)(2,1)} async-done(((bf16[4,128,2048]{2,1,0:T(8,128)(2,1)}), bf16[4,128,2048]{2,1,0:T(8,128)(2,1)}, u32[]{:S(2)}, u32[]{:S(2)}) %all-to-all-start.1) | async-done | bytes 2097184 | tf_op jit(solution)/shard_map/all_to_all | solution.py:72
  668.5 52.4 %all_to_all.100 = bf16[4,128,2048]{2,1,0:T(8,128)(2,1)} all-to-all(bf16[4,128,2048]{2,1,0:T(8,128)(2,1)} %bitcast.231), channel_id=1, replica_groups=mesh['seq'=4,'ctx'=4,'fsdp'=2] {'ctx'}, dimensions={0} | all-to-all | bytes 4194304 | tf_op jit(solution)/shard_map/all_to_all | solution.py:72
  724.3 8.0 all-to-all-done.6
  736.8 17.3 %all-to-all-done.8 = bf16[4,64,1536]{2,1,0:T(8,128)(2,1)} async-done(((bf16[4,64,1536]{2,1,0:T(8,128)(2,1)}), bf16[4,64,1536]{2,1,0:T(8,128)(2,1)}, u32[]{:S(2)}, u32[]{:S(2)}) %all-to-all-start.8) | async-done | bytes 786464 | tf_op jit(solution)/shard_map/all_to_all | solution.py:83
  761.2 41.2 %all-reduce.1 = (f32[2048]{0:T(1024)}, f32[128]{0:T(128)}, f32[128]{0:T(128)}, f32[2048]{0:T(1024)}) all-reduce(f32[2048]{0:T(1024)S(1)} %get-tuple-element.26, f32[128]{0:T(128)S(1)} %get-tuple-element.10, f32[128]{0:T(128)S(1)} %get-tuple-element.14, ...), channel_id=1, replica_groups=mesh['seq'=4,'ctx'=4,'fsdp'=2] {'seq','ctx','fsdp'}, use_global_device_ids=true, to_apply=%region_16.17 | all-reduce | flops 4352 | bytes 34816 | tf_op jit(solution)/shard_map/psum | solution.py:253
  819.8 27.4 %all-to-all-done.7 = bf16[4,64,3072]{2,1,0:T(8,128)(2,1)} async-done(((bf16[4,64,3072]{2,1,0:T(8,128)(2,1)}), bf16[4,64,3072]{2,1,0:T(8,128)(2,1)}, u32[]{:S(2)}, u32[]{:S(2)}) %all-to-all-start.7) | async-done | bytes 1572896 | tf_op jit(solution)/shard_map/all_to_all | solution.py:83
  (246 shorter events, 188.5 us)
Async XLA Ops:
  7.2 156.9 %copy-start = (bf16[256,6144]{1,0:T(8,128)(2,1)S(1)}, bf16[256,6144]{1,0:T(8,128)(2,1)}, u32[]{:S(2)}) copy-start(bf16[256,6144]{1,0:T(8,128)(2,1)} %param.20) | copy-start | bytes 9437188
  7.2 50.8 %all-gather.24.cloned.1.call-start = ((), (), s32[]{:S(2)}) async-start(), calls=%async_computation.23 | async-start | bytes 2621440 | tf_op jit(solution)/shard_map/all_gather | solution.py:63
  8.0 87.9 %all-gather.12.cloned.1.call-start = ((), (), s32[]{:S(2)}) async-start(), calls=%async_computation.13 | async-start | bytes 4718592 | tf_op jit(solution)/shard_map/all_gather | solution.py:67
  10.1 85.7 %copy-start.40 = (f32[2048]{0:T(1024)S(1)}, f32[2048]{0:T(1024)}, u32[]{:S(2)}) copy-start(f32[2048]{0:T(1024)} %param.13) | copy-start | bytes 24580
  11.0 141.0 %all-gather.14.cloned.1.call-start = ((), (), s32[]{:S(2)}) async-start(), calls=%async_computation.14 | async-start | bytes 9437184 | tf_op jit(solution)/shard_map/all_gather | solution.py:67
  11.8 194.6 %all-gather.16.cloned.1.call-start = ((), (), s32[]{:S(2)}) async-start(), calls=%async_computation.15 | async-start | bytes 2621440 | tf_op jit(solution)/shard_map/all_gather | solution.py:63
  160.5 118.9 %all-gather.18.cloned.1.call-start = ((), (), s32[]{:S(2)}) async-start(), calls=%async_computation.16 | async-start | bytes 14155776 | tf_op jit(solution)/shard_map/all_gather | solution.py:67
  163.4 163.1 %all-gather.26.cloned.1.call-start = ((), (), s32[]{:S(2)}) async-start(), calls=%async_computation.24 | async-start | bytes 2621440 | tf_op jit(solution)/shard_map/all_gather | solution.py:63
  164.0 209.3 %all-gather.20.cloned.1.call-start = ((), (), s32[]{:S(2)}) async-start(), calls=%async_computation.17 | async-start | bytes 7077888 | tf_op jit(solution)/shard_map/all_gather | solution.py:67
  165.0 325.4 %all-gather.22.cloned.1.call-start = ((), (), s32[]{:S(2)}) async-start(), calls=%async_computation.19 | async-start | bytes 2621440 | tf_op jit(solution)/shard_map/all_gather | solution.py:63
  391.1 53.5 %copy-start.5 = (f32[128,2048]{1,0:T(8,128)S(1)}, f32[128,2048]{1,0:T(8,128)}, u32[]{:S(2)}) copy-start(f32[128,2048]{1,0:T(8,128)} %copy-done.4) | copy-start | bytes 3145732
  444.7 45.7 %copy-start.29 = (bf16[2,128,2,512]{3,1,2,0:T(8,128)(2,1)S(1)}, bf16[2,128,2,512]{3,1,2,0:T(8,128)(2,1)}, u32[]{:S(2)}) copy-start(bf16[2,128,2,512]{3,1,2,0:T(8,128)(2,1)} %convolution_convert_fusion.7) | copy-start | bytes 1572868
  446.5 274.4 %reduce-scatter.7.cloned.1.call-start = ((), (), s32[]{:S(2)}) async-start(), calls=%async_computation.20 | async-start | bytes 2359296 | tf_op jit(solution)/shard_map/reduce_scatter | solution.py:82
  494.9 229.4 %reduce-scatter.11.cloned.1.call-start = ((), (), s32[]{:S(2)}) async-start(), calls=%async_computation.22 | async-start | bytes 7077888 | tf_op jit(solution)/shard_map/reduce_scatter | solution.py:82
  519.0 13.1 %copy-start.20 = (f32[512,128]{0,1:T(8,128)S(1)}, f32[512,128]{0,1:T(8,128)}, u32[]{:S(2)}) copy-start(f32[512,128]{0,1:T(8,128)} %get-tuple-element.47) | copy-start | bytes 786436
  526.6 18.8 %all-to-all-start.3 = ((bf16[128,4,512]{0,2,1:T(8,128)(2,1)}), bf16[128,4,512]{0,2,1:T(8,128)(2,1)}, u32[]{:S(2)}, u32[]{:S(2)}) async-start(bf16[128,4,512]{0,2,1:T(8,128)(2,1)} %bitcast.26), calls=%async_computation.3 | async-start | bytes 1048576 | tf_op jit(solution)/shard_map/all_to_all | solution.py:212
  530.8 206.0 %reduce-scatter.5.cloned.1.call-start = ((), (), s32[]{:S(2)}) async-start(), calls=%async_computation.18 | async-start | bytes 4718592 | tf_op jit(solution)/shard_map/reduce_scatter | solution.py:82
  592.1 213.7 %reduce-scatter.9.cloned.1.call-start = ((), (), s32[]{:S(2)}) async-start(), calls=%async_computation.21 | async-start | bytes 14155776 | tf_op jit(solution)/shard_map/reduce_scatter | solution.py:82
  615.6 52.9 %all-to-all-start.1 = ((bf16[4,128,2048]{2,1,0:T(8,128)(2,1)}), bf16[4,128,2048]{2,1,0:T(8,128)(2,1)}, u32[]{:S(2)}, u32[]{:S(2)}) async-start(bf16[4,128,2048]{2,1,0:T(8,128)(2,1)} %bitcast.230), calls=%async_computation.1 | async-start | bytes 4194304 | tf_op jit(solution)/shard_map/all_to_all | solution.py:72
  668.5 68.0 %copy-start.8 = (bf16[1,128,2048]{2,1,0:T(8,128)(2,1)S(1)}, bf16[1,128,2048]{2,1,0:T(8,128)(2,1)}, u32[]{:S(2)}) copy-start(bf16[1,128,2048]{2,1,0:T(8,128)(2,1)} %param.11) | copy-start | bytes 1572868
  720.9 11.5 %all-to-all-start.6 = ((bf16[4,64,512]{2,1,0:T(8,128)(2,1)}), bf16[4,64,512]{2,1,0:T(8,128)(2,1)S(1)}, u32[]{:S(2)}, u32[]{:S(2)}) async-start(bf16[4,64,512]{2,1,0:T(8,128)(2,1)} %bitcast.250), calls=%async_computation.8 | async-start | bytes 524288 | tf_op jit(solution)/shard_map/all_to_all | solution.py:83
  732.3 21.7 %all-to-all-start.8 = ((bf16[4,64,1536]{2,1,0:T(8,128)(2,1)}), bf16[4,64,1536]{2,1,0:T(8,128)(2,1)}, u32[]{:S(2)}, u32[]{:S(2)}) async-start(bf16[4,64,1536]{2,1,0:T(8,128)(2,1)} %bitcast.243), calls=%async_computation.12 | async-start | bytes 1572864 | tf_op jit(solution)/shard_map/all_to_all | solution.py:83
  754.1 51.8 %all-to-all-start.5 = ((bf16[4,64,1024]{2,1,0:T(8,128)(2,1)}), bf16[4,64,1024]{2,1,0:T(8,128)(2,1)}, u32[]{:S(2)}, u32[]{:S(2)}) async-start(bf16[4,64,1024]{2,1,0:T(8,128)(2,1)} %bitcast.246), calls=%async_computation.6 | async-start | bytes 1048576 | tf_op jit(solution)/shard_map/all_to_all | solution.py:83
  805.9 41.3 %all-to-all-start.7 = ((bf16[4,64,3072]{2,1,0:T(8,128)(2,1)}), bf16[4,64,3072]{2,1,0:T(8,128)(2,1)}, u32[]{:S(2)}, u32[]{:S(2)}) async-start(bf16[4,64,3072]{2,1,0:T(8,128)(2,1)} %bitcast.239), calls=%async_computation.10 | async-start | bytes 3145728 | tf_op jit(solution)/shard_map/all_to_all | solution.py:83
  (42 other events, 170.0 us)
Sparse Core Ops, SparseCore 0:
  9.6 48.4 all-gather.23
  60.5 35.2 all-gather.11
  97.7 54.2 all-gather.13
  160.6 45.6 all-gather.15
  208.6 70.7 all-gather.17
  280.9 45.6 all-gather.25
  329.0 44.1 all-gather.19
  446.6 43.7 all-gather.21
  495.0 39.9 reduce-scatter.6
  538.2 61.7 reduce-scatter.10
  603.4 51.1 reduce-scatter.4
  657.9 92.2 reduce-scatter.8
where the time goes:
time: 868 us; the launch traced here: 859 us
  waiting for transfers between devices  419 us (48%)
  blocking collectives  176 us (20%)
  matrix products  101 us (12%)
  local copies, waits for them, and re-layouts  79.5 us (9%)
  other arithmetic  40.4 us (5%)
  starting transfers between devices  25.9 us (3%)
  between operations  15.9 us (2%)
    all_gather x4, waiting for transfers between devices, gather_plane(): return lax.all_gather(rows, PLANE, axis=0, tiled=True)  159 us
    all_gather x4, waiting for transfers between devices, gather_ctx(): return lax.all_gather(rows, 'ctx', axis=0, tiled=True)  153 us
    all_to_all x2, blocking collectives, scatter_ctx(): pieces = lax.all_to_all(partials.astype(BF16), 'ctx', 0, 0, tiled=True)  106 us
    all_to_all x4, waiting for transfers between devices, scatter_weight(): grad = lax.all_to_all(grad, 'ctx', 0, 0, tiled=True)  52.7 us
    all_to_all x1, waiting for transfers between devices, scatter_ctx(): pieces = lax.all_to_all(partials.astype(BF16), 'ctx', 0, 0, tiled=True)  41.7 us
    psum x1, blocking collectives, local(): lax.psum((attention_part, query_part, key_part, feedforward_part), ('seq'...  41.2 us
    dot_general x4, matrix products, rows_by(): return jnp.dot(left, right, preferred_element_type=F32)  33.6 us
    dot_general x4, matrix products, rows_by_t(): lax.dot_general(left, right, (((1,), (1,)), ((), ())), preferred_element_...  28.5 us
  transfers between devices with their start and end apart: 18, of which 13 were waited for; matrix products, arithmetic and copies ran while one was open for 21% of the time, Pallas kernels for 0%

commit v1 on v0

--- a/solution.py
+++ b/solution.py
@@ -16,6 +16,18 @@
 BF16 = jnp.bfloat16
 
 
+def doubled_up(x, axis, dim):
+    ways, here = (lax.axis_size(axis), lax.axis_index(axis))
+    grown, reach = (x, 1)
+    while reach < ways:
+        theirs = lax.ppermute(grown, axis, [(d, d ^ reach) for d in range(ways)])
+        mine_first = jnp.concatenate([grown, theirs], axis=dim)
+        theirs_first = jnp.concatenate([theirs, grown], axis=dim)
+        grown = jnp.where(here & reach == 0, mine_first, theirs_first)
+        reach = 2 * reach
+    return grown
+
+
 def rms_scale(values):
     return lax.rsqrt(jnp.mean(values * values, axis=-1, keepdims=True) + EPS)
 
@@ -60,7 +72,7 @@
 
 
 def gather_ctx(rows):
-    return lax.all_gather(rows, "ctx", axis=0, tiled=True)
+    return doubled_up(rows, "ctx", 0)
 
 
 def gather_plane(rows):

time: 868 us -> 731 us (0.84)
  waiting for transfers between devices: 419 us -> 281 us
  local copies, waits for them, and re-layouts: 79.5 us -> 62.7 us
  blocking collectives: 176 us -> 189 us
    ppermute x0 -> x8, waiting for transfers between devices: none -> 185 us  [doubled_up(): theirs = lax.ppermute(grown, axis, [(d, d ^ reach) for d in range(ways)])]
    all_gather x4, waiting for transfers between devices: 159 us -> 1.94 us  [gather_plane(): return lax.all_gather(rows, PLANE, axis=0, tiled=True)]
    all_gather x4 -> x0, waiting for transfers between devices: 153 us -> none  [gather_ctx(): return lax.all_gather(rows, 'ctx', axis=0, tiled=True)]
    all_to_all x0 -> x1, blocking collectives: none -> 11.3 us  [scatter_weight(): grad = lax.all_to_all(grad, 'ctx', 0, 0, tiled=True)]
    ppermute x0 -> x8, starting transfers between devices: none -> 8.94 us  [doubled_up(): theirs = lax.ppermute(grown, axis, [(d, d ^ reach) for d in range(ways)])]
    convert_element_type x1 -> x0, local copies, waits for them, and re-layouts: 8.75 us -> none  [scatter_weight(): grad = grad.astype(BF16).reshape(seqs, ctxs, cores, rows, grad.shape[1])]
    all_to_all x4 -> x3, waiting for transfers between devices: 52.7 us -> 45.4 us  [scatter_weight(): grad = lax.all_to_all(grad, 'ctx', 0, 0, tiled=True)]
  transfers between devices with their start and end apart: 18 -> 21, of which waited for: 13 -> 12; matrix products, arithmetic and copies ran while one was open for 21% -> 23% of each run, Pallas kernels for 0% -> 0%
where the time goes in v1:
time: 731 us; the launch traced here: 721 us
  waiting for transfers between devices  281 us (38%)
  blocking collectives  189 us (26%)
  matrix products  104 us (14%)
  local copies, waits for them, and re-layouts  62.7 us (9%)
  other arithmetic  37.2 us (5%)
  starting transfers between devices  31.2 us (4%)
  between operations  16.2 us (2%)
    ppermute x8, waiting for transfers between devices, doubled_up(): theirs = lax.ppermute(grown, axis, [(d, d ^ reach) for d in range(ways)])  185 us
    all_to_all x2, blocking collectives, scatter_ctx(): pieces = lax.all_to_all(partials.astype(BF16), 'ctx', 0, 0, tiled=True)  105 us
    all_to_all x3, waiting for transfers between devices, scatter_weight(): grad = lax.all_to_all(grad, 'ctx', 0, 0, tiled=True)  45.4 us
    all_to_all x1, waiting for transfers between devices, scatter_ctx(): pieces = lax.all_to_all(partials.astype(BF16), 'ctx', 0, 0, tiled=True)  40.5 us
    psum x1, blocking collectives, local(): lax.psum((attention_part, query_part, key_part, feedforward_part), ('seq'...  40.1 us
    dot_general x4, matrix products, rows_by(): return jnp.dot(left, right, preferred_element_type=F32)  36.8 us
    dot_general x4, matrix products, rows_by_t(): lax.dot_general(left, right, (((1,), (1,)), ((), ())), preferred_element_...  32 us
    dot_general x4, matrix products, t_by_rows(): lax.dot_general(left, right, (((0,), (0,)), ((), ())), preferred_element_...  19.8 us
  transfers between devices with their start and end apart: 21, of which 12 were waited for; matrix products, arithmetic and copies ran while one was open for 23% of the time, Pallas kernels for 0%

profile of v1, /device:TPU:0, one launch (start us, length us, event | category | flops | bytes accessed | tf_op | source)
XLA Modules:
  0.0 721.2 jit_solution(14190479509304898441)
XLA Ops:
  19.5 14.3 %all-reduce = s32[8]{0:T(128)S(1)} all-reduce(s32[8]{0:T(128)S(1)} %bitcast_dynamic-update-slice_fusion), channel_id=2, replica_groups=mesh['seq'=4,'ctx'=4,'fsdp'=2] {'ctx'}, use_global_device_ids=true, to_apply=%add | all-reduce | flops 8 | bytes 64
  38.4 44.0 %collective-permute-done.1 = bf16[256,2048]{1,0:T(8,128)(2,1)S(1)} collective-permute-done((bf16[256,2048]{1,0:T(8,128)(2,1)S(1)}, bf16[256,2048]{1,0:T(8,128)(2,1)S(1)}, u32[]{:S(2)}, u32[]{:S(2)}) %collective-permute-start.1) | collective-permute-done | bytes 1048608 | tf_op jit(solution)/shard_map/ppermute | solution.py:23
  97.0 17.6 %all_to_all.98 = bf16[4,128,512]{1,2,0:T(8,128)(2,1)} all-to-all(bf16[4,128,512]{1,2,0:T(8,128)(2,1)S(1)} %copy.195), channel_id=1, replica_groups=mesh['seq'=4,'ctx'=4,'fsdp'=2] {'ctx'}, dimensions={0} | all-to-all | bytes 1048576 | tf_op jit(solution)/shard_map/all_to_all | solution.py:197
  114.6 7.7 %multiply_reduce_fusion.5 = (f32[128]{0:T(128)S(1)}, f32[128,2048]{1,0:T(8,128)S(1)}) fusion(bf16[128,2048]{0,1:T(8,128)(2,1)} %bitcast.220, bf16[2048,2048]{1,0:T(8,128)(2,1)} %all-gather.8.cloned.1.call-done, bf16[1,128,2048]{2,1,0:T(8,128)(2,1)S(1)} %copy-done.5), kind=kOutput, calls=%fused_computation.86 | convolution fusion | flops 1074790272 | bytes 10486272 | tf_op jit(solution)/shard_map/dot_general | solution.py:67
  122.5 12.0 %collective-permute-done.2 = bf16[128,2048]{1,0:T(8,128)(2,1)S(1)} collective-permute-done((bf16[128,2048]{1,0:T(8,128)(2,1)S(1)}, bf16[128,2048]{1,0:T(8,128)(2,1)S(1)}, u32[]{:S(2)}, u32[]{:S(2)}) %collective-permute-start.2) | collective-permute-done | bytes 524320 | tf_op jit(solution)/shard_map/ppermute | solution.py:23
  137.0 30.6 %collective-permute-done.4 = bf16[128,2048]{1,0:T(8,128)(2,1)S(1)} collective-permute-done((bf16[128,2048]{1,0:T(8,128)(2,1)S(1)}, bf16[128,2048]{1,0:T(8,128)(2,1)S(1)}, u32[]{:S(2)}, u32[]{:S(2)}) %collective-permute-start.4) | collective-permute-done | bytes 524320 | tf_op jit(solution)/shard_map/ppermute | solution.py:23
  171.4 32.1 %collective-permute-done.3 = bf16[256,2048]{1,0:T(8,128)(2,1)} collective-permute-done((bf16[256,2048]{1,0:T(8,128)(2,1)S(1)}, bf16[256,2048]{1,0:T(8,128)(2,1)}, u32[]{:S(2)}, u32[]{:S(2)}) %collective-permute-start.3) | collective-permute-done | bytes 1048608 | tf_op jit(solution)/shard_map/ppermute | solution.py:23
  203.5 14.3 %fusion.40 = f32[512,3072]{1,0:T(8,128)} fusion(bf16[2048,3072]{1,0:T(8,128)(2,1)} %all-gather.10.cloned.1.call-done, bf16[256,2048]{1,0:T(8,128)(2,1)} %collective-permute-done.3, bf16[256,2048]{1,0:T(8,128)(2,1)} %copy-done.31, pred[]{:T(512)S(6)} %eq.4), kind=kOutput, calls=%fused_computation.113 | convolution fusion | flops 6451888128 | bytes 20971520 | tf_op jit(solution)/shard_map/dot_general | solution.py:63
  217.8 7.9 %collective-permute-done.5 = bf16[256,2048]{1,0:T(8,128)(2,1)S(1)} collective-permute-done((bf16[256,2048]{1,0:T(8,128)(2,1)}, bf16[256,2048]{1,0:T(8,128)(2,1)S(1)}, u32[]{:S(2)}, u32[]{:S(2)}) %collective-permute-start.5) | collective-permute-done | bytes 1048608 | tf_op jit(solution)/shard_map/ppermute | solution.py:23
  227.6 12.0 %multiply_convert_fusion.1 = (bf16[512,1536]{1,0:T(8,128)(2,1)}, bf16[512,1536]{1,0:T(8,128)(2,1)}, bf16[512,1536]{1,0:T(8,128)(2,1)}) fusion(f32[512,3072]{1,0:T(8,128)} %fusion.40, bf16[2048,1536]{1,0:T(8,128)(2,1)} %all-gather.12.cloned.1.call-done, bf16[256,2048]{1,0:T(8,128)(2,1)S(1)} %collective-permute-done.5, ...), kind=kOutput, calls=%fused_computation.22 | convolution fusion | flops 3242459136 | bytes 19398656 | tf_op jit(solution)/shard_map/dot_general | solution.py:63
  239.6 8.7 %convolution_convert_fusion.3 = bf16[512,2048]{1,0:T(8,128)(2,1)S(1)} fusion(bf16[2048,3072]{1,0:T(8,128)(2,1)S(1)} %copy-done.44, bf16[512,1536]{1,0:T(8,128)(2,1)} %get-tuple-element.22, bf16[512,1536]{1,0:T(8,128)(2,1)} %get-tuple-element.21), kind=kOutput, calls=%fused_computation.26 | convolution fusion | flops 6449790976 | bytes 17825792 | tf_op jit(solution)/shard_map/dot_general | solution.py:67
  248.4 53.0 %all_to_all.99 = bf16[4,128,2048]{2,1,0:T(8,128)(2,1)S(1)} all-to-all(bf16[4,128,2048]{2,1,0:T(8,128)(2,1)S(1)} %bitcast.214), channel_id=1, replica_groups=mesh['seq'=4,'ctx'=4,'fsdp'=2] {'ctx'}, dimensions={0} | all-to-all | bytes 4194304 | tf_op jit(solution)/shard_map/all_to_all | solution.py:84
  303.1 12.7 %collective-permute-done.6 = bf16[128,2048]{1,0:T(8,128)(2,1)S(1)} collective-permute-done((bf16[128,2048]{1,0:T(8,128)(2,1)S(1)}, bf16[128,2048]{1,0:T(8,128)(2,1)S(1)}, u32[]{:S(2)}, u32[]{:S(2)}) %collective-permute-start.6) | collective-permute-done | bytes 524320 | tf_op jit(solution)/shard_map/ppermute | solution.py:23
  316.8 45.9 %collective-permute-done.7 = bf16[256,2048]{1,0:T(8,128)(2,1)S(1)} collective-permute-done((bf16[256,2048]{1,0:T(8,128)(2,1)S(1)}, bf16[256,2048]{1,0:T(8,128)(2,1)S(1)}, u32[]{:S(2)}, u32[]{:S(2)}) %collective-permute-start.7) | collective-permute-done | bytes 1048608 | tf_op jit(solution)/shard_map/ppermute | solution.py:23
  394.6 7.5 %all-to-all-done.3 = bf16[128,4,512]{0,2,1:T(8,128)(2,1)} async-done(((bf16[128,4,512]{0,2,1:T(8,128)(2,1)}), bf16[128,4,512]{0,2,1:T(8,128)(2,1)}, u32[]{:S(2)}, u32[]{:S(2)}) %all-to-all-start.3) | async-done | bytes 524320 | tf_op jit(solution)/shard_map/all_to_all | solution.py:224
  455.6 9.2 %convolution_convert_fusion = bf16[2048,3072]{1,0:T(8,128)(2,1)S(1)} fusion(bf16[512,1536]{1,0:T(8,128)(2,1)} %get-tuple-element.22, bf16[512,1536]{1,0:T(8,128)(2,1)} %get-tuple-element.21, bf16[256,2048]{1,0:T(8,128)(2,1)} %collective-permute-done.3, bf16[256,2048]{1,0:T(8,128)(2,1)S(1)} %copy-done.32, pred[]{:T(512)S(6)} %eq.4), kind=kOutput, calls=%fused_computation | convolution fusion | flops 6464471040 | bytes 17825792 | tf_op jit(solution)/shard_map/dot_general | solution.py:71
  470.5 8.1 %convolution_convert_fusion.5 = bf16[512,2048]{1,0:T(8,128)(2,1)} fusion(bf16[512,1536]{1,0:T(8,128)(2,1)} %get-tuple-element.23, bf16[2048,1536]{1,0:T(8,128)(2,1)} %all-gather.12.cloned.1.call-done), kind=kOutput, calls=%fused_computation.28 | convolution fusion | flops 3222274048 | bytes 9961472 | tf_op jit(solution)/shard_map/dot_general | solution.py:67
  483.2 7.6 %fusion.3 = (f32[2048]{0:T(1024)S(1)}, bf16[512,2048]{1,0:T(8,128)(2,1)}) fusion(f32[512]{0:T(512)S(1)} %add_rsqrt_fusion.2, bf16[256,2048]{1,0:T(8,128)(2,1)S(1)} %copy-done.19, bf16[256,2048]{1,0:T(8,128)(2,1)} %copy-done.34, pred[]{:T(512)S(6)} %eq.4, bf16[2048,1024]{1,0:T(8,128)(2,1)} %all-gather.6.cloned.1.call-done, ...), kind=kOutput, calls=%fused_computation.7 | convolution fusion | flops 2165307392 | bytes 9447425 | tf_op jit(solution)/shard_map/dot_general | solution.py:67
  490.8 40.5 %all-to-all-done.1 = bf16[4,128,2048]{2,1,0:T(8,128)(2,1)} async-done(((bf16[4,128,2048]{2,1,0:T(8,128)(2,1)}), bf16[4,128,2048]{2,1,0:T(8,128)(2,1)}, u32[]{:S(2)}, u32[]{:S(2)}) %all-to-all-start.1) | async-done | bytes 2097184 | tf_op jit(solution)/shard_map/all_to_all | solution.py:84
  531.3 52.3 %all_to_all.100 = bf16[4,128,2048]{2,1,0:T(8,128)(2,1)} all-to-all(bf16[4,128,2048]{2,1,0:T(8,128)(2,1)} %bitcast.212), channel_id=1, replica_groups=mesh['seq'=4,'ctx'=4,'fsdp'=2] {'ctx'}, dimensions={0} | all-to-all | bytes 4194304 | tf_op jit(solution)/shard_map/all_to_all | solution.py:84
  583.7 11.3 %all_to_all.101 = bf16[4,64,512]{2,1,0:T(8,128)(2,1)S(1)} all-to-all(bf16[4,64,512]{2,1,0:T(8,128)(2,1)} %bitcast.232), channel_id=1, replica_groups=mesh['seq'=4,'ctx'=4,'fsdp'=2] {'ctx'}, dimensions={0} | all-to-all | bytes 524288 | tf_op jit(solution)/shard_map/all_to_all | solution.py:95
  599.3 18.0 %all-to-all-done.8 = bf16[4,64,1536]{2,1,0:T(8,128)(2,1)} async-done(((bf16[4,64,1536]{2,1,0:T(8,128)(2,1)}), bf16[4,64,1536]{2,1,0:T(8,128)(2,1)}, u32[]{:S(2)}, u32[]{:S(2)}) %all-to-all-start.8) | async-done | bytes 786464 | tf_op jit(solution)/shard_map/all_to_all | solution.py:95
  624.5 40.1 %all-reduce.1 = (f32[2048]{0:T(1024)}, f32[128]{0:T(128)}, f32[128]{0:T(128)}, f32[2048]{0:T(1024)}) all-reduce(f32[2048]{0:T(1024)S(1)} %get-tuple-element.26, f32[128]{0:T(128)S(1)} %get-tuple-element.10, f32[128]{0:T(128)S(1)} %get-tuple-element.14, ...), channel_id=1, replica_groups=mesh['seq'=4,'ctx'=4,'fsdp'=2] {'seq','ctx','fsdp'}, use_global_device_ids=true, to_apply=%region_16.17 | all-reduce | flops 4352 | bytes 34816 | tf_op jit(solution)/shard_map/psum | solution.py:265
  682.0 27.4 %all-to-all-done.7 = bf16[4,64,3072]{2,1,0:T(8,128)(2,1)} async-done(((bf16[4,64,3072]{2,1,0:T(8,128)(2,1)}), bf16[4,64,3072]{2,1,0:T(8,128)(2,1)}, u32[]{:S(2)}, u32[]{:S(2)}) %all-to-all-start.7) | async-done | bytes 1572896 | tf_op jit(solution)/shard_map/all_to_all | solution.py:95
  (252 shorter events, 170.3 us)
Async XLA Ops:
  7.2 75.9 %all-gather.6.cloned.1.call-start = ((), (), s32[]{:S(2)}) async-start(), calls=%async_computation.13 | async-start | bytes 4718592 | tf_op jit(solution)/shard_map/all_gather | solution.py:79
  10.3 104.3 %all-gather.8.cloned.1.call-start = ((), (), s32[]{:S(2)}) async-start(), calls=%async_computation.14 | async-start | bytes 9437184 | tf_op jit(solution)/shard_map/all_gather | solution.py:79
  11.0 192.4 %all-gather.10.cloned.1.call-start = ((), (), s32[]{:S(2)}) async-start(), calls=%async_computation.15 | async-start | bytes 14155776 | tf_op jit(solution)/shard_map/all_gather | solution.py:79
  13.9 213.7 %all-gather.12.cloned.1.call-start = ((), (), s32[]{:S(2)}) async-start(), calls=%async_computation.16 | async-start | bytes 7077888 | tf_op jit(solution)/shard_map/all_gather | solution.py:79
  14.0 19.8 %collective-permute-start = (bf16[128,2048]{1,0:T(8,128)(2,1)}, bf16[128,2048]{1,0:T(8,128)(2,1)}, u32[]{:S(2)}, u32[]{:S(2)}) collective-permute-start(bf16[128,2048]{1,0:T(8,128)(2,1)} %bitcast.193), channel_id=1, source_target_pairs={{0,2},{2,0},{4,6},{6,4},{1,3},{3,1},{5,7},{7,5},{8,10},{10,8},{12,... | collective-permute-start | bytes 1572872 | tf_op jit(solution)/shard_map/ppermute | solution.py:23
  19.4 63.7 %copy-start.41 = (f32[2048]{0:T(1024)S(1)}, f32[2048]{0:T(1024)}, u32[]{:S(2)}) copy-start(f32[2048]{0:T(1024)} %param.13) | copy-start | bytes 24580
  19.4 564.3 %reduce-scatter.7.cloned.1.call-start = ((), (), s32[]{:S(2)}) async-start(), calls=%async_computation.18 | async-start | bytes 2359296 | tf_op jit(solution)/shard_map/reduce_scatter | solution.py:94
  36.0 46.3 %collective-permute-start.1 = (bf16[256,2048]{1,0:T(8,128)(2,1)S(1)}, bf16[256,2048]{1,0:T(8,128)(2,1)S(1)}, u32[]{:S(2)}, u32[]{:S(2)}) collective-permute-start(bf16[256,2048]{1,0:T(8,128)(2,1)S(1)} %maximum_select_fusion.5), channel_id=1, source_target_pairs={{0,4},{2,6},{4,0},{6,2},{1,5},{3,7},{5,1},{7,3},{8,12},{10,14},{12... | collective-permute-start | bytes 3145736 | tf_op jit(solution)/shard_map/ppermute | solution.py:23
  122.4 12.1 %collective-permute-start.2 = (bf16[128,2048]{1,0:T(8,128)(2,1)S(1)}, bf16[128,2048]{1,0:T(8,128)(2,1)S(1)}, u32[]{:S(2)}, u32[]{:S(2)}) collective-permute-start(bf16[128,2048]{1,0:T(8,128)(2,1)S(1)} %multiply_convert_fusion.3), channel_id=1, source_target_pairs={{0,2},{2,0},{4,6},{6,4},{1,3},{3,1},{5,7},{7,5},{8,10},{10,8},{12,... | collective-permute-start | bytes 1572872 | tf_op jit(solution)/shard_map/ppermute | solution.py:23
  134.8 68.6 %collective-permute-start.3 = (bf16[256,2048]{1,0:T(8,128)(2,1)S(1)}, bf16[256,2048]{1,0:T(8,128)(2,1)}, u32[]{:S(2)}, u32[]{:S(2)}) collective-permute-start(bf16[256,2048]{1,0:T(8,128)(2,1)S(1)} %maximum_select_fusion.6), channel_id=1, source_target_pairs={{0,4},{2,6},{4,0},{6,2},{1,5},{3,7},{5,1},{7,3},{8,12},{10,14},{12... | collective-permute-start | bytes 3145736 | tf_op jit(solution)/shard_map/ppermute | solution.py:23
  135.3 32.4 %collective-permute-start.4 = (bf16[128,2048]{1,0:T(8,128)(2,1)S(1)}, bf16[128,2048]{1,0:T(8,128)(2,1)S(1)}, u32[]{:S(2)}, u32[]{:S(2)}) collective-permute-start(bf16[128,2048]{1,0:T(8,128)(2,1)S(1)} %bitcast.200), channel_id=1, source_target_pairs={{0,2},{2,0},{4,6},{6,4},{1,3},{3,1},{5,7},{7,5},{8,10},{10,8},{12,... | collective-permute-start | bytes 1572872 | tf_op jit(solution)/shard_map/ppermute | solution.py:23
  168.9 56.8 %collective-permute-start.5 = (bf16[256,2048]{1,0:T(8,128)(2,1)}, bf16[256,2048]{1,0:T(8,128)(2,1)S(1)}, u32[]{:S(2)}, u32[]{:S(2)}) collective-permute-start(bf16[256,2048]{1,0:T(8,128)(2,1)} %maximum_select_fusion.7), channel_id=1, source_target_pairs={{0,4},{2,6},{4,0},{6,2},{1,5},{3,7},{5,1},{7,3},{8,12},{10,14},{12... | collective-permute-start | bytes 3145736 | tf_op jit(solution)/shard_map/ppermute | solution.py:23
  302.1 60.5 %copy-start.30 = (bf16[2,128,2,512]{3,1,2,0:T(8,128)(2,1)S(1)}, bf16[2,128,2,512]{3,1,2,0:T(8,128)(2,1)}, u32[]{:S(2)}) copy-start(bf16[2,128,2,512]{3,1,2,0:T(8,128)(2,1)} %copy-done.29) | copy-start | bytes 1572868
  302.8 13.0 %collective-permute-start.6 = (bf16[128,2048]{1,0:T(8,128)(2,1)S(1)}, bf16[128,2048]{1,0:T(8,128)(2,1)S(1)}, u32[]{:S(2)}, u32[]{:S(2)}) collective-permute-start(bf16[128,2048]{1,0:T(8,128)(2,1)S(1)} %fusion.56), channel_id=1, source_target_pairs={{0,2},{2,0},{4,6},{6,4},{1,3},{3,1},{5,7},{7,5},{8,10},{10,8},{12,... | collective-permute-start | bytes 1572872 | tf_op jit(solution)/shard_map/ppermute | solution.py:23
  316.1 46.6 %collective-permute-start.7 = (bf16[256,2048]{1,0:T(8,128)(2,1)S(1)}, bf16[256,2048]{1,0:T(8,128)(2,1)S(1)}, u32[]{:S(2)}, u32[]{:S(2)}) collective-permute-start(bf16[256,2048]{1,0:T(8,128)(2,1)S(1)} %maximum_select_fusion.8), channel_id=1, source_target_pairs={{0,4},{2,6},{4,0},{6,2},{1,5},{3,7},{5,1},{7,3},{8,12},{10,14},{12... | collective-permute-start | bytes 3145736 | tf_op jit(solution)/shard_map/ppermute | solution.py:23
  365.5 229.5 %reduce-scatter.11.cloned.1.call-start = ((), (), s32[]{:S(2)}) async-start(), calls=%async_computation.20 | async-start | bytes 7077888 | tf_op jit(solution)/shard_map/reduce_scatter | solution.py:94
  382.9 19.2 %all-to-all-start.3 = ((bf16[128,4,512]{0,2,1:T(8,128)(2,1)}), bf16[128,4,512]{0,2,1:T(8,128)(2,1)}, u32[]{:S(2)}, u32[]{:S(2)}) async-start(bf16[128,4,512]{0,2,1:T(8,128)(2,1)} %bitcast.217), calls=%async_computation.3 | async-start | bytes 1048576 | tf_op jit(solution)/shard_map/all_to_all | solution.py:224
  387.1 212.2 %reduce-scatter.5.cloned.1.call-start = ((), (), s32[]{:S(2)}) async-start(), calls=%async_computation.17 | async-start | bytes 4718592 | tf_op jit(solution)/shard_map/reduce_scatter | solution.py:94
  454.4 213.6 %reduce-scatter.9.cloned.1.call-start = ((), (), s32[]{:S(2)}) async-start(), calls=%async_computation.19 | async-start | bytes 14155776 | tf_op jit(solution)/shard_map/reduce_scatter | solution.py:94
  478.5 52.8 %all-to-all-start.1 = ((bf16[4,128,2048]{2,1,0:T(8,128)(2,1)}), bf16[4,128,2048]{2,1,0:T(8,128)(2,1)}, u32[]{:S(2)}, u32[]{:S(2)}) async-start(bf16[4,128,2048]{2,1,0:T(8,128)(2,1)} %bitcast.211), calls=%async_computation.1 | async-start | bytes 4194304 | tf_op jit(solution)/shard_map/all_to_all | solution.py:84
  531.3 67.8 %copy-start.6 = (bf16[1,128,2048]{2,1,0:T(8,128)(2,1)S(1)}, bf16[1,128,2048]{2,1,0:T(8,128)(2,1)}, u32[]{:S(2)}) copy-start(bf16[1,128,2048]{2,1,0:T(8,128)(2,1)} %param.11) | copy-start | bytes 1572868
  594.9 22.4 %all-to-all-start.8 = ((bf16[4,64,1536]{2,1,0:T(8,128)(2,1)}), bf16[4,64,1536]{2,1,0:T(8,128)(2,1)}, u32[]{:S(2)}, u32[]{:S(2)}) async-start(bf16[4,64,1536]{2,1,0:T(8,128)(2,1)} %bitcast.225), calls=%async_computation.12 | async-start | bytes 1572864 | tf_op jit(solution)/shard_map/all_to_all | solution.py:95
  617.3 50.7 %all-to-all-start.5 = ((bf16[4,64,1024]{2,1,0:T(8,128)(2,1)}), bf16[4,64,1024]{2,1,0:T(8,128)(2,1)}, u32[]{:S(2)}, u32[]{:S(2)}) async-start(bf16[4,64,1024]{2,1,0:T(8,128)(2,1)} %bitcast.228), calls=%async_computation.6 | async-start | bytes 1048576 | tf_op jit(solution)/shard_map/all_to_all | solution.py:95
  668.1 41.3 %all-to-all-start.7 = ((bf16[4,64,3072]{2,1,0:T(8,128)(2,1)}), bf16[4,64,3072]{2,1,0:T(8,128)(2,1)}, u32[]{:S(2)}, u32[]{:S(2)}) async-start(bf16[4,64,3072]{2,1,0:T(8,128)(2,1)} %bitcast.221), calls=%async_computation.10 | async-start | bytes 3145728 | tf_op jit(solution)/shard_map/all_to_all | solution.py:95
  (45 other events, 289.6 us)
Sparse Core Ops, SparseCore 0:
  10.5 39.2 all-gather.5
  51.7 54.2 all-gather.7
  108.5 71.9 all-gather.9
  182.2 45.3 all-gather.11
  365.6 39.9 reduce-scatter.6
  408.8 61.7 reduce-scatter.10
  473.9 51.1 reduce-scatter.4
  528.6 92.2 reduce-scatter.8
